TPU v7x, 32 devices: a whole 2x2x4 slice. The times are simulated.
32 devices in a mesh: table: 16 (over z, y, x), narrow: 2 (over core).
Axes of the slice: x: 2, y: 2, z: 4, core: 2. Of those that a mesh axis runs over, the one named last changes fastest.
Arguments:
- table_rows: bfloat16 [16384, 256], P('table'), may hold values from -3 to 3
- accum: float32 [16384], P('table'), may hold values from 1 to 100
- factor_down: bfloat16 [2048, 256], P('narrow'), may hold values from -0.125 to 0.125
- factor_up: bfloat16 [2048, 256], P('narrow'), may hold values from -0.375 to 0.375
- cross_bias: float32 [2048], replicated, may hold values from -3 to 3
- out_weight: bfloat16 [2048], replicated, may hold values from -0.125 to 0.125
- target: float32 [4096], P(('table', 'narrow')), may hold values from 0 to 1
- bag_rows: int32 [512, 512], P(('table', 'narrow')), may hold values from -1 to 1023, as said below
- slot_target: int32 [512, 128], P(('table', 'narrow')), may hold values from -1 to 1023, as said below
Outputs:
- logits: float32 [4096], P(('table', 'narrow'))
- down_grad: float32 [2048, 256], P('narrow')
- up_grad: float32 [2048, 256], P('narrow')
- new_rows: bfloat16 [16384, 256], P('table')
- new_accum: float32 [16384], P(('table', 'narrow'))
Inputs may be any that keep to these rules, and one draw needn't show every extreme that they name: `slot_target`: for each source device (its 16 rows): every bag 0 .. 1023 is named by exactly one slot and the other slots hold -1; in every draw each source device has one window all of whose 128 slots are used. `bag_rows`: A used slot holds 1 to 4 rows of the window first and -1 after them; an unused slot holds -1 only; each source device has a slot with 4 lookups.
All inputs are finite; a program needn't handle non-finite values.
Results may differ from a plain program's by a relative error of at most 0.0077.
Values may be sent and summed in bfloat16 or wider, within the bound.
No kernel may reach another device: no remote copies, remote signals or barrier semaphores. Data moves between devices by JAX's collectives and lax.ppermute only.
A program may use at most 64 MiB of HBM per device.

v0:
```python
import math
import jax
import jax.numpy as jnp
from jax import lax
from jax.sharding import PartitionSpec as P

FEAT = 8
HOT = 4
LEARN_RATE = 0.2
LOSS_SCALE = 32.0
ADA_EPS = 1e-06


def transposed_dot(left, right):
    return lax.dot_general(
        left, right, (((0,), (0,)), ((), ())), preferred_element_type=jnp.float32
    )


def rows_dot(left, right):
    return lax.dot_general(
        left, right, (((1,), (1,)), ((), ())), preferred_element_type=jnp.float32
    )


def local(
    table_rows, accum, factor_down, factor_up, cross_bias, out_weight, target, bag_rows, slot_target
):
    tables = lax.axis_size("table")
    narrows = lax.axis_size("narrow")
    row_dev, emb_width = table_rows.shape
    pools_per = slot_target.shape[1]
    samples = target.shape[0]
    bag_count = samples * FEAT
    slot_count = tables * pools_per
    asked = lax.all_to_all(bag_rows, "table", split_axis=0, concat_axis=0, tiled=True)
    lookup_ids = asked.reshape(slot_count, HOT)
    positions = lax.broadcasted_iota(jnp.int32, (1, row_dev), 1)
    counts = jnp.zeros((slot_count, row_dev), jnp.bfloat16)
    for lookup in range(HOT):
        counts = counts + (lookup_ids[:, lookup : lookup + 1] == positions).astype(jnp.bfloat16)
    pool_sums = jnp.dot(counts, table_rows, preferred_element_type=jnp.float32)
    pool_out = pool_sums.astype(jnp.bfloat16).reshape(tables, pools_per, emb_width)
    arrived = lax.all_to_all(pool_out, "table", split_axis=0, concat_axis=0, tiled=True).reshape(
        slot_count, emb_width
    )
    bag_index = lax.broadcasted_iota(jnp.int32, (bag_count, 1), 0)
    placing = (slot_target.reshape(1, slot_count) == bag_index).astype(jnp.bfloat16)
    pooled_feats = (
        jnp.dot(placing, arrived, preferred_element_type=jnp.float32)
        .astype(jnp.bfloat16)
        .reshape(samples, FEAT * emb_width)
    )
    down_full, up_full = (
        lax.all_gather(factor_down, "narrow", axis=0, tiled=True),
        lax.all_gather(factor_up, "narrow", axis=0, tiled=True),
    )
    hidden = jnp.dot(pooled_feats, down_full, preferred_element_type=jnp.float32).astype(
        jnp.bfloat16
    )
    cross_out = rows_dot(hidden, up_full)
    feats_f = pooled_feats.astype(jnp.float32)
    shifted = cross_out + cross_bias
    mixed_out = feats_f * shifted + feats_f
    weight_f = out_weight.astype(jnp.float32)
    logits = jnp.sum(mixed_out * weight_f, axis=1)
    dlogit = LOSS_SCALE * (jax.nn.sigmoid(logits) - target)
    dmixed = dlogit[:, None] * weight_f
    dcross = (dmixed * feats_f).astype(jnp.bfloat16)
    dhidden = jnp.dot(dcross, up_full, preferred_element_type=jnp.float32).astype(jnp.bfloat16)
    back_term = rows_dot(dhidden, down_full)
    dpooled = (dmixed * (shifted + 1.0) + back_term).astype(jnp.bfloat16)
    narrow_sum = lax.psum_scatter(
        jnp.concatenate(
            [transposed_dot(pooled_feats, dhidden), transposed_dot(dcross, hidden)], axis=1
        ).astype(jnp.bfloat16),
        "narrow",
        scatter_dimension=0,
        tiled=True,
    ).astype(jnp.float32)
    grand_total = lax.psum(narrow_sum, "table")
    batch_all = samples * tables * narrows
    grand_total = grand_total * (1.0 / math.sqrt(batch_all))
    rank_size = factor_down.shape[1]
    down_grad = grand_total[:, :rank_size]
    up_grad = grand_total[:, rank_size:]
    bag_grads = dpooled.reshape(bag_count, emb_width)
    slot_grads = (
        transposed_dot(placing, bag_grads)
        .astype(jnp.bfloat16)
        .reshape(tables, pools_per, emb_width)
    )
    returned = lax.all_to_all(slot_grads, "table", split_axis=0, concat_axis=0, tiled=True).reshape(
        slot_count, emb_width
    )
    local_grad = transposed_dot(counts, returned)
    narrow_index = lax.axis_index("narrow")
    share_size = row_dev // narrows
    row_grad = lax.psum(local_grad.astype(jnp.bfloat16), "narrow").astype(jnp.float32)
    accum_all = accum + jnp.mean(row_grad * row_grad, axis=1)
    new_rows = (
        table_rows.astype(jnp.float32)
        - LEARN_RATE * row_grad * lax.rsqrt(accum_all + ADA_EPS)[:, None]
    ).astype(jnp.bfloat16)
    new_accum = lax.dynamic_slice_in_dim(accum_all, narrow_index * share_size, share_size, 0)
    return (logits, down_grad, up_grad, new_rows, new_accum)


def solution(mesh):
    in_specs = (
        P("table", None),
        P("table"),
        P("narrow", None),
        P("narrow", None),
        P(),
        P(),
        P(("table", "narrow")),
        P(("table", "narrow"), None),
        P(("table", "narrow"), None),
    )
    out_specs = (
        P(("table", "narrow")),
        P("narrow", None),
        P("narrow", None),
        P("table", None),
        P(("table", "narrow")),
    )
    return jax.shard_map(local, mesh=mesh, in_specs=in_specs, out_specs=out_specs, check_vma=False)
```

profile of v0, /device:TPU:0, one launch (start us, length us, event | category | flops | bytes accessed | tf_op | source)
XLA Modules:
  0.0 247.3 jit_solution(3443778541291321474)
XLA Ops:
  7.2 0.8 all_to_all.12
  8.0 15.5 %all_to_all.19 = s32[16,1,512]{2,1,0:T(1,128)S(1)} all-to-all(s32[16,1,512]{2,1,0:T(1,128)S(1)} %all_to_all.12), channel_id=1, replica_groups=mesh['table'=16,'narrow'=2] {'table'}, dimensions={0} | all-to-all | bytes 65536 | tf_op jit(solution)/shard_map/all_to_all | solution.py:36
  23.5 0.1 reduce
  23.5 1.1 reshape.40
  24.6 0.0 copy-start.2
  24.6 2.0 slice_reduce_fusion.3
  26.6 0.0 copy-done.2
  26.6 6.1 %fusion.15 = bf16[2048,256]{1,0:T(8,128)(2,1)} fusion(bf16[1024,256]{1,0:T(8,128)(2,1)S(1)} %copy-done.2, s32[2048]{0:T(1024)S(1)} %get-tuple-element.21, s32[2048]{0:T(1024)S(1)} %get-tuple-element.22, s32[2048]{0:T(1024)S(1)} %get-tuple-element.23, s32[2048]{0:T(1024)S(1)} %get-tuple-element.20), kind=kOutput, calls=%fused_computation.18 | convolution fusion | flops 1107820544 | bytes 1605632 | tf_op jit(solution)/shard_map/dot_general | solution.py:42
  32.7 3.8 %all-to-all-start.1 = ((bf16[16,128,256]{2,1,0:T(8,128)(2,1)}), bf16[16,128,256]{2,1,0:T(8,128)(2,1)S(1)}, u32[]{:S(2)}, u32[]{:S(2)}) async-start(bf16[16,128,256]{2,1,0:T(8,128)(2,1)} %bitcast.1), calls=%async_computation.1 | async-start | bytes 2097152 | tf_op jit(solution)/shard_map/all_to_all | solution.py:44
  36.5 0.0 all-gather.3.cloned.1.call-start
  36.5 0.7 all-gather.3.cloned.1.call-update
  37.2 0.0 all-gather.5.cloned.1.call-start
  37.3 0.7 all-gather.5.cloned.1.call-update
  38.0 21.7 %all-to-all-done.1 = bf16[16,128,256]{2,1,0:T(8,128)(2,1)S(1)} async-done(((bf16[16,128,256]{2,1,0:T(8,128)(2,1)}), bf16[16,128,256]{2,1,0:T(8,128)(2,1)S(1)}, u32[]{:S(2)}, u32[]{:S(2)}) %all-to-all-start.1) | async-done | bytes 1048608 | tf_op jit(solution)/shard_map/all_to_all | solution.py:44
  59.8 1.5 fusion.23
  61.2 0.0 copy-start.3
  61.2 0.2 reshape.43
  61.5 0.0 copy-start.8
  61.5 0.0 all-gather.3.cloned.1.call-done
  61.5 1.5 convolution_convert_fusion.3
  63.1 0.0 all-gather.5.cloned.1.call-done
  63.1 2.0 fusion.29
  65.1 0.0 copy-start.6
  65.1 0.4 convolution_convert_fusion.2
  65.5 0.0 copy-done
  65.5 0.5 fusion.19
  66.0 0.2 reshape.44
  66.3 3.3 %fusion.18 = bf16[2048,256]{1,0:T(8,128)(2,1)} fusion(bf16[1024,256]{1,0:T(8,128)(2,1)S(1)} %reshape.44, s32[2048]{0:T(1024)S(1)} %bitcast.22), kind=kOutput, calls=%fused_computation.19 | convolution fusion | flops 1076363264 | bytes 1581056 | tf_op jit(solution)/shard_map/dot_general | solution.py:15
  69.6 5.8 %all-to-all-start.2 = ((bf16[16,128,256]{2,1,0:T(8,128)(2,1)}), bf16[16,128,256]{2,1,0:T(8,128)(2,1)S(1)}, u32[]{:S(2)}, u32[]{:S(2)}) async-start(bf16[16,128,256]{2,1,0:T(8,128)(2,1)} %bitcast.3), calls=%async_computation.3 | async-start | bytes 2097152 | tf_op jit(solution)/shard_map/all_to_all | solution.py:93
  75.4 0.2 all-reduce.3.cloned.1.call-start
  75.6 0.5 convolution_convert_fusion
  76.2 23.0 %all-to-all-done.2 = bf16[16,128,256]{2,1,0:T(8,128)(2,1)S(1)} async-done(((bf16[16,128,256]{2,1,0:T(8,128)(2,1)}), bf16[16,128,256]{2,1,0:T(8,128)(2,1)S(1)}, u32[]{:S(2)}, u32[]{:S(2)}) %all-to-all-start.2) | async-done | bytes 1048608 | tf_op jit(solution)/shard_map/all_to_all | solution.py:93
  99.1 5.5 %fusion.20 = bf16[1024,256]{1,0:T(8,128)(2,1)} fusion(bf16[2048,256]{1,0:T(8,128)(2,1)S(1)} %bitcast.20, s32[2048]{0:T(1024)S(1)} %get-tuple-element.21, s32[2048]{0:T(1024)S(1)} %get-tuple-element.22, s32[2048]{0:T(1024)S(1)} %get-tuple-element.23, s32[2048]{0:T(1024)S(1)} %get-tuple-element.20), kind=kOutput, calls=%fused_computation.31 | convolution fusion | flops 1107558400 | bytes 1605632 | tf_op jit(solution)/shard_map/dot_general | solution.py:15
  104.6 0.0 all-reduce.3.cloned.1.call-update
  104.6 0.0 reduce-scatter.2.cloned.1.call-start
  104.7 0.5 convolution_convert_fusion.1
  105.2 1.5 pad_maximum_fusion
  106.7 0.0 reduce-scatter.2.cloned.1.call-update
  106.7 17.0 %all-reduce.3.cloned.1.call-done = bf16[1024,256]{1,0:T(8,128)(2,1)} async-done(((bf16[1024,256]{1,0:T(8,128)(2,1)}), bf16[1024,256]{1,0:T(8,128)(2,1)}) %all-reduce.3.cloned.1.call-update) | async-done | bytes 524304 | tf_op jit(solution)/shard_map/psum | solution.py:99
  123.7 1.3 fusion.24
  125.0 0.7 dynamic_slice.3
  125.7 2.1 fusion.26
  127.8 8.9 %reduce-scatter.2.cloned.1.call-done = bf16[1024,512]{0,1:T(8,128)(2,1)} async-done(((bf16[2048,512]{0,1:T(8,128)(2,1)}), bf16[1024,512]{0,1:T(8,128)(2,1)}) %reduce-scatter.2.cloned.1.call-update) | async-done | bytes 1048592 | tf_op jit(solution)/shard_map/reduce_scatter | solution.py:73
  136.7 100.9 %all-reduce.4 = f32[1024,512]{0,1:T(8,128)S(1)} all-reduce(bf16[1024,512]{0,1:T(8,128)(2,1)} %reduce-scatter.2.cloned.1.call-done), channel_id=1, replica_groups=mesh['table'=16,'narrow'=2] {'table'}, use_global_device_ids=true, to_apply=%region_2.0 | all-reduce | flops 524288 | bytes 3145728 | tf_op jit(solution)/shard_map/psum | solution.py:81
  237.7 0.2 broadcast_multiply_fusion
  237.9 0.2 fusion.33
  238.2 1.3 copy.19
  239.5 1.3 copy.18
  (15 shorter events, 0.0 us)
Async XLA Ops:
  24.6 2.0 copy-start.2
  32.7 5.3 %copy-start.4 = (bf16[2048]{0:T(1024)(128)(2,1)S(1)}, bf16[2048]{0:T(1024)(128)(2,1)}, u32[]{:S(2)}) copy-start(bf16[2048]{0:T(1024)(128)(2,1)} %param.14) | copy-start | bytes 12292
  32.7 27.1 %copy-start.7 = (s32[16,128]{1,0:T(8,128)S(1)}, s32[16,128]{1,0:T(8,128)}, u32[]{:S(2)}) copy-start(s32[16,128]{1,0:T(8,128)} %param.17) | copy-start | bytes 24580
  32.7 27.1 %all-to-all-start.1 = ((bf16[16,128,256]{2,1,0:T(8,128)(2,1)}), bf16[16,128,256]{2,1,0:T(8,128)(2,1)S(1)}, u32[]{:S(2)}, u32[]{:S(2)}) async-start(bf16[16,128,256]{2,1,0:T(8,128)(2,1)} %bitcast.1), calls=%async_computation.1 | async-start | bytes 2097152 | tf_op jit(solution)/shard_map/all_to_all | solution.py:44
  36.5 25.0 %all-gather.3.cloned.1.call-start = ((), (), s32[]{:S(2)}) async-start(), calls=%async_computation.4 | async-start | bytes 1572864 | tf_op jit(solution)/shard_map/all_gather | solution.py:55
  37.2 25.9 %all-gather.5.cloned.1.call-start = ((), (), s32[]{:S(2)}) async-start(), calls=%async_computation.5 | async-start | bytes 1572864 | tf_op jit(solution)/shard_map/all_gather | solution.py:56
  61.2 1.9 copy-start.3
  61.5 3.6 %copy-start.8 = (f32[128]{0:T(128)S(1)}, f32[128]{0:T(128)}, u32[]{:S(2)}) copy-start(f32[128]{0:T(128)} %param.15) | copy-start | bytes 1540
  63.1 2.4 copy-start
  63.1 2.0 copy-start.1
  65.1 0.9 copy-start.6
  69.6 29.5 %all-to-all-start.2 = ((bf16[16,128,256]{2,1,0:T(8,128)(2,1)}), bf16[16,128,256]{2,1,0:T(8,128)(2,1)S(1)}, u32[]{:S(2)}, u32[]{:S(2)}) async-start(bf16[16,128,256]{2,1,0:T(8,128)(2,1)} %bitcast.3), calls=%async_computation.3 | async-start | bytes 2097152 | tf_op jit(solution)/shard_map/all_to_all | solution.py:93
  75.4 48.3 %all-reduce.3.cloned.1.call-start = ((), (), s32[]{:S(2)}) async-start(), calls=%async_computation.7 | async-start | bytes 1048576 | tf_op jit(solution)/shard_map/psum | solution.py:99
  104.6 32.1 %reduce-scatter.2.cloned.1.call-start = ((), (), s32[]{:S(2)}) async-start(), calls=%async_computation.6 | async-start | bytes 3145728 | tf_op jit(solution)/shard_map/reduce_scatter | solution.py:73
  106.7 18.3 %copy-start.5 = (f32[1024]{0:T(1024)S(1)}, f32[1024]{0:T(1024)}, u32[]{:S(2)}) copy-start(f32[1024]{0:T(1024)} %param.10) | copy-start | bytes 12292
Sparse Core Ops, SparseCore 0:
  38.9 10.2 all-gather.2
  50.7 10.1 all-gather.4
  104.8 18.9 all-reduce.2
  125.9 10.7 reduce-scatter.1
where the time goes:
time: 248 us; the launch traced here: 247 us
  blocking collectives  116 us (47%)
  waiting for transfers between devices  72.1 us (29%)
  matrix products  21.7 us (9%)
  between operations  14 us (6%)
  starting transfers between devices  9.95 us (4%)
  local copies, waits for them, and re-layouts  7.88 us (3%)
  other arithmetic  5.22 us (2%)
    psum x1, blocking collectives, local(): grand_total = lax.psum(narrow_sum, 'table')  101 us
    all_to_all x1, waiting for transfers between devices, local(): lax.all_to_all(slot_grads, 'table', split_axis=0, concat_axis=0, tiled=True)  23 us
    all_to_all x1, waiting for transfers between devices, local(): lax.all_to_all(pool_out, 'table', split_axis=0, concat_axis=0, tiled=True)  21.7 us
    psum x1, waiting for transfers between devices, local(): lax.psum(local_grad.astype(jnp.bfloat16), 'narrow').astype(jnp.float32)  17 us
    all_to_all x1, blocking collectives, local(): lax.all_to_all(bag_rows, 'table', split_axis=0, concat_axis=0, tiled=True)  15.5 us
    dot_general x4, matrix products, transposed_dot(): lax.dot_general(left, right, (((0,), (0,)), ((), ())), preferred_element_...  9.82 us
    reduce_scatter x1, waiting for transfers between devices, local(): lax.psum_scatter(jnp.concatenate([transposed_dot(pooled_feats, dhidden),...  8.95 us
    dot_general x1, matrix products, local(): pool_sums = jnp.dot(counts, table_rows, preferred_element_type=jnp.float32)  6.07 us
  transfers between devices with their start and end apart: 6, of which 4 were waited for; matrix products, arithmetic and copies ran while one was open for 4% of the time, Pallas kernels for 0%

commit v1 on v0

--- a/solution.py
+++ b/solution.py
@@ -9,6 +9,11 @@
 LEARN_RATE = 0.2
 LOSS_SCALE = 32.0
 ADA_EPS = 1e-06
+
+
+def gather_and_add(value, axis):
+    parts = lax.all_gather(value, axis)
+    return jnp.sum(parts, axis=0)
 
 
 def transposed_dot(left, right):
@@ -96,7 +101,7 @@
     local_grad = transposed_dot(counts, returned)
     narrow_index = lax.axis_index("narrow")
     share_size = row_dev // narrows
-    row_grad = lax.psum(local_grad.astype(jnp.bfloat16), "narrow").astype(jnp.float32)
+    row_grad = gather_and_add(local_grad.astype(jnp.bfloat16), "narrow").astype(jnp.float32)
     accum_all = accum + jnp.mean(row_grad * row_grad, axis=1)
     new_rows = (
         table_rows.astype(jnp.float32)

time: 248 us -> 238 us (0.960)
  waiting for transfers between devices: 72.1 us -> 37.2 us
  blocking collectives: 116 us -> 149 us
  starting transfers between devices: 9.95 us -> 3.95 us
    all_to_all x0 -> x1, blocking collectives: none -> 31.3 us  [local(): lax.all_to_all(slot_grads, 'table', split_axis=0, concat_axis=0, tiled=True)]
    all_to_all x1 -> x0, waiting for transfers between devices: 23 us -> none  [local(): lax.all_to_all(slot_grads, 'table', split_axis=0, concat_axis=0, tiled=True)]
    psum x1 -> x0, waiting for transfers between devices: 17 us -> none  [local(): lax.psum(local_grad.astype(jnp.bfloat16), 'narrow').astype(jnp.float32)]
    all_to_all x1 -> x0, starting transfers between devices: 5.82 us -> none  [local(): lax.all_to_all(slot_grads, 'table', split_axis=0, concat_axis=0, tiled=True)]
    all_gather x0 -> x1, waiting for transfers between devices: none -> 4.78 us  [gather_and_add(): parts = lax.all_gather(value, axis)]
  transfers between devices with their start and end apart: 6 -> 5, of which waited for: 4 -> 3; matrix products, arithmetic and copies ran while one was open for 4% -> 4% of each run, Pallas kernels for 0% -> 0%
where the time goes in v1:
time: 238 us; the launch traced here: 237 us
  blocking collectives  149 us (63%)
  waiting for transfers between devices  37.2 us (16%)
  matrix products  20.7 us (9%)
  between operations  14 us (6%)
  local copies, waits for them, and re-layouts  7.88 us (3%)
  other arithmetic  4.89 us (2%)
  starting transfers between devices  3.95 us (2%)
    psum x1, blocking collectives, local(): grand_total = lax.psum(narrow_sum, 'table')  102 us
    all_to_all x1, blocking collectives, local(): lax.all_to_all(slot_grads, 'table', split_axis=0, concat_axis=0, tiled=True)  31.3 us
    all_to_all x1, waiting for transfers between devices, local(): lax.all_to_all(pool_out, 'table', split_axis=0, concat_axis=0, tiled=True)  21.7 us
    all_to_all x1, blocking collectives, local(): lax.all_to_all(bag_rows, 'table', split_axis=0, concat_axis=0, tiled=True)  15.5 us
    reduce_scatter x1, waiting for transfers between devices, local(): lax.psum_scatter(jnp.concatenate([transposed_dot(pooled_feats, dhidden),...  9.23 us
    dot_general x4, matrix products, transposed_dot(): lax.dot_general(left, right, (((0,), (0,)), ((), ())), preferred_element_...  8.9 us
    dot_general x1, matrix products, local(): pool_sums = jnp.dot(counts, table_rows, preferred_element_type=jnp.float32)  6.07 us
    all_gather x1, waiting for transfers between devices, gather_and_add(): parts = lax.all_gather(value, axis)  4.78 us
  transfers between devices with their start and end apart: 5, of which 3 were waited for; matrix products, arithmetic and copies ran while one was open for 4% of the time, Pallas kernels for 0%

profile of v1, /device:TPU:0, one launch (start us, length us, event | category | flops | bytes accessed | tf_op | source)
XLA Modules:
  0.0 237.3 jit_solution(7463739314771961278)
XLA Ops:
  7.2 0.8 all_to_all.12
  8.0 15.5 %all_to_all.19 = s32[16,1,512]{2,1,0:T(1,128)S(1)} all-to-all(s32[16,1,512]{2,1,0:T(1,128)S(1)} %all_to_all.12), channel_id=1, replica_groups=mesh['table'=16,'narrow'=2] {'table'}, dimensions={0} | all-to-all | bytes 65536 | tf_op jit(solution)/shard_map/all_to_all | solution.py:41
  23.5 0.1 reduce.1
  23.5 1.1 reshape.40
  24.6 0.0 copy-start.2
  24.6 2.0 slice_reduce_fusion.3
  26.6 6.1 %fusion.15 = bf16[2048,256]{1,0:T(8,128)(2,1)} fusion(bf16[1024,256]{1,0:T(8,128)(2,1)S(1)} %copy-done.2, s32[2048]{0:T(1024)S(1)} %get-tuple-element.21, s32[2048]{0:T(1024)S(1)} %get-tuple-element.22, s32[2048]{0:T(1024)S(1)} %get-tuple-element.23, s32[2048]{0:T(1024)S(1)} %get-tuple-element.20), kind=kOutput, calls=%fused_computation.18 | convolution fusion | flops 1107820544 | bytes 1605632 | tf_op jit(solution)/shard_map/dot_general | solution.py:47
  32.7 3.8 %all-to-all-start.1 = ((bf16[16,128,256]{2,1,0:T(8,128)(2,1)}), bf16[16,128,256]{2,1,0:T(8,128)(2,1)S(1)}, u32[]{:S(2)}, u32[]{:S(2)}) async-start(bf16[16,128,256]{2,1,0:T(8,128)(2,1)} %bitcast.1), calls=%async_computation.1 | async-start | bytes 2097152 | tf_op jit(solution)/shard_map/all_to_all | solution.py:49
  36.5 0.0 all-gather.5.cloned.1.call-start
  36.5 0.7 all-gather.5.cloned.1.call-update
  37.2 0.0 all-gather.7.cloned.1.call-start
  37.3 0.7 all-gather.7.cloned.1.call-update
  38.0 0.0 all-gather.9.cloned.1.call-start
  38.0 21.7 %all-to-all-done.1 = bf16[16,128,256]{2,1,0:T(8,128)(2,1)S(1)} async-done(((bf16[16,128,256]{2,1,0:T(8,128)(2,1)}), bf16[16,128,256]{2,1,0:T(8,128)(2,1)S(1)}, u32[]{:S(2)}, u32[]{:S(2)}) %all-to-all-start.1) | async-done | bytes 1048608 | tf_op jit(solution)/shard_map/all_to_all | solution.py:49
  59.8 1.5 fusion.23
  61.2 0.0 copy-start.3
  61.2 0.2 reshape.43
  61.5 0.0 copy-start.8
  61.5 0.0 all-gather.5.cloned.1.call-done
  61.5 1.5 convolution_convert_fusion.3
  63.1 0.0 copy-start
  63.1 0.0 all-gather.7.cloned.1.call-done
  63.1 2.0 fusion.29
  65.1 0.0 copy-start.6
  65.1 0.0 copy-done.8
  65.1 0.4 convolution_convert_fusion.2
  65.5 0.5 fusion.19
  66.0 0.2 reshape.44
  66.3 2.4 fusion.18
  68.6 31.3 %all_to_all.20 = bf16[16,128,256]{2,1,0:T(8,128)(2,1)S(1)} all-to-all(bf16[16,128,256]{2,1,0:T(8,128)(2,1)S(1)} %bitcast.23), channel_id=1, replica_groups=mesh['table'=16,'narrow'=2] {'table'}, dimensions={0} | all-to-all | bytes 2097152 | tf_op jit(solution)/shard_map/all_to_all | solution.py:98
  99.9 5.5 %fusion.20 = bf16[1024,256]{1,0:T(8,128)(2,1)} fusion(bf16[2048,256]{1,0:T(8,128)(2,1)S(1)} %bitcast.22, s32[2048]{0:T(1024)S(1)} %get-tuple-element.21, s32[2048]{0:T(1024)S(1)} %get-tuple-element.22, s32[2048]{0:T(1024)S(1)} %get-tuple-element.23, s32[2048]{0:T(1024)S(1)} %get-tuple-element.20), kind=kOutput, calls=%fused_computation.31 | convolution fusion | flops 1107558400 | bytes 1605632 | tf_op jit(solution)/shard_map/dot_general | solution.py:20
  105.5 0.0 all-gather.9.cloned.1.call-update
  105.5 0.0 reduce-scatter.2.cloned.1.call-start
  105.5 0.5 convolution_convert_fusion.1
  106.0 0.5 convolution_convert_fusion
  106.5 1.6 pad_maximum_fusion
  108.1 0.0 reduce-scatter.2.cloned.1.call-update
  108.2 4.8 %all-gather.9.cloned.1.call-done = bf16[2048,256]{1,0:T(8,128)(2,1)} async-done(((bf16[1024,256]{1,0:T(8,128)(2,1)}), bf16[2048,256]{1,0:T(8,128)(2,1)}) %all-gather.9.cloned.1.call-update) | async-done | bytes 1048592 | tf_op jit(solution)/shard_map/all_gather | solution.py:15
  112.9 1.7 reduce_sum.31
  114.6 0.2 fusion.24
  114.9 0.7 dynamic_slice.3
  115.5 1.1 fusion.26
  116.6 9.2 %reduce-scatter.2.cloned.1.call-done = bf16[1024,512]{0,1:T(8,128)(2,1)} async-done(((bf16[2048,512]{0,1:T(8,128)(2,1)}), bf16[1024,512]{0,1:T(8,128)(2,1)}) %reduce-scatter.2.cloned.1.call-update) | async-done | bytes 1048592 | tf_op jit(solution)/shard_map/reduce_scatter | solution.py:78
  125.8 101.9 %all-reduce.1 = f32[1024,512]{0,1:T(8,128)S(1)} all-reduce(bf16[1024,512]{0,1:T(8,128)(2,1)} %reduce-scatter.2.cloned.1.call-done), channel_id=1, replica_groups=mesh['table'=16,'narrow'=2] {'table'}, use_global_device_ids=true, to_apply=%region_2.0 | all-reduce | flops 524288 | bytes 3145728 | tf_op jit(solution)/shard_map/psum | solution.py:86
  227.7 0.2 broadcast_multiply_fusion
  227.9 0.2 fusion.33
  228.2 1.3 copy.19
  229.5 1.3 copy.18
  (15 shorter events, 0.0 us)
Async XLA Ops:
  24.6 2.0 copy-start.2
  32.7 5.3 %copy-start.4 = (bf16[2048]{0:T(1024)(128)(2,1)S(1)}, bf16[2048]{0:T(1024)(128)(2,1)}, u32[]{:S(2)}) copy-start(bf16[2048]{0:T(1024)(128)(2,1)} %param.14) | copy-start | bytes 12292
  32.7 27.1 %copy-start.7 = (s32[16,128]{1,0:T(8,128)S(1)}, s32[16,128]{1,0:T(8,128)}, u32[]{:S(2)}) copy-start(s32[16,128]{1,0:T(8,128)} %param.17) | copy-start | bytes 24580
  32.7 27.1 %all-to-all-start.1 = ((bf16[16,128,256]{2,1,0:T(8,128)(2,1)}), bf16[16,128,256]{2,1,0:T(8,128)(2,1)S(1)}, u32[]{:S(2)}, u32[]{:S(2)}) async-start(bf16[16,128,256]{2,1,0:T(8,128)(2,1)} %bitcast.1), calls=%async_computation.1 | async-start | bytes 2097152 | tf_op jit(solution)/shard_map/all_to_all | solution.py:49
  36.5 25.0 %all-gather.5.cloned.1.call-start = ((), (), s32[]{:S(2)}) async-start(), calls=%async_computation.4 | async-start | bytes 1572864 | tf_op jit(solution)/shard_map/all_gather | solution.py:60
  37.2 25.9 %all-gather.7.cloned.1.call-start = ((), (), s32[]{:S(2)}) async-start(), calls=%async_computation.5 | async-start | bytes 1572864 | tf_op jit(solution)/shard_map/all_gather | solution.py:61
  38.0 75.0 %all-gather.9.cloned.1.call-start = ((), (), s32[]{:S(2)}) async-start(), calls=%async_computation.7 | async-start | bytes 1572864 | tf_op jit(solution)/shard_map/all_gather | solution.py:15
  61.2 1.9 copy-start.3
  61.5 3.6 %copy-start.8 = (f32[128]{0:T(128)S(1)}, f32[128]{0:T(128)}, u32[]{:S(2)}) copy-start(f32[128]{0:T(128)} %param.15) | copy-start | bytes 1540
  63.1 2.4 %copy-start = (bf16[2048,256]{1,0:T(8,128)(2,1)S(1)}, bf16[2048,256]{1,0:T(8,128)(2,1)}, u32[]{:S(2)}) copy-start(bf16[2048,256]{1,0:T(8,128)(2,1)} %all-gather.5.cloned.1.call-done) | copy-start | bytes 3145732
  63.1 2.0 copy-start.1
  65.1 0.9 copy-start.6
  105.5 20.4 %reduce-scatter.2.cloned.1.call-start = ((), (), s32[]{:S(2)}) async-start(), calls=%async_computation.6 | async-start | bytes 3145728 | tf_op jit(solution)/shard_map/reduce_scatter | solution.py:78
  108.1 6.7 %copy-start.5 = (f32[1024]{0:T(1024)S(1)}, f32[1024]{0:T(1024)}, u32[]{:S(2)}) copy-start(f32[1024]{0:T(1024)} %param.10) | copy-start | bytes 12292
Sparse Core Ops, SparseCore 0:
  38.9 10.2 all-gather.4
  50.7 10.1 all-gather.6
  105.6 7.2 all-gather.8
  115.0 10.7 reduce-scatter.1
